TPU v7x, 512 devices: a whole 4x8x8 slice. The times are simulated.
512 devices in a mesh: tm: 8 (over x, z_hi), vert: 64 (over y, z_lo, core).
Axes of the slice: x: 4, y: 8, z: 8 (z_hi: 2, z_lo: 4; z = z_hi * 4 + z_lo), core: 2. Of those that a mesh axis runs over, the one named last changes fastest.
Arguments:
- frames: bfloat16 [16, 8192, 256], P('tm', 'vert'), may hold values from -12 to 12
- cotangent: bfloat16 [16, 8192, 256], P('tm', 'vert'), may hold values from -200 to 200
- table: int32 [8192, 7], P('vert'), may hold values from -1 to 8191, as said below
- w_conv: bfloat16 [1792, 256], replicated, may hold values from -0.125 to 0.125
- w_attn: bfloat16 [4, 256, 256], replicated, may hold values from -0.375 to 0.375
Outputs:
- grad_frames: bfloat16 [16, 8192, 256], P('tm', 'vert')
- grad_conv: bfloat16 [1792, 256], replicated
- grad_attn: bfloat16 [4, 256, 256], replicated
Inputs may be any that keep to these rules, and one draw needn't show every extreme that they name: `table`: each entry of row v is -1 (an empty slot) or a vertex at most 64 places from v in the vertex order; slot 0 is v itself; some entries lie exactly 64 places away on either side.
All inputs are finite; a program needn't handle non-finite values.
Results may differ from a plain program's by a relative error of at most 0.014.
The roundings to bfloat16 on the way count: a program that leaves them out, or rounds other values in their place, can miss the bound.
Values may be sent and summed in bfloat16 or wider, within the bound.
No kernel may reach another device: no remote copies, remote signals or barrier semaphores. Data moves between devices by JAX's collectives and lax.ppermute only.
A program may use at most 64 MiB of HBM per device.

v0:
```python
import functools
import math

import jax
import jax.numpy as jnp
from jax import lax
from jax.experimental import pallas as pl
from jax.experimental.pallas import tpu as pltpu
from jax.sharding import PartitionSpec as P


TF = 16
HEADS = 8
HW = 64
TM = ("x_hi", "x_lo", "z_hi")
VERT = ("y_hi", "y_lo", "z_mid", "z_lo", "core")
PAIR = "core"
NEAR = ("x_lo", "y_lo", "z_lo")
FAR = ("x_hi", "z_hi", "y_hi", "z_mid")
TILE = 16
BF = jnp.bfloat16
F32 = jnp.float32

LIMIT = pltpu.CompilerParams(vmem_limit_bytes=32 * 1024 * 1024)


def mm(left, right):
    return jnp.dot(left, right, preferred_element_type=F32)


def mm_nt(left, right):
    return lax.dot_general(left, right, (((1,), (1,)), ((), ())), preferred_element_type=F32)


def mm_tn(left, right):
    return lax.dot_general(left, right, (((0,), (0,)), ((), ())), preferred_element_type=F32)


def slot_places(table):
    lanes = lax.broadcasted_iota(jnp.int32, table.shape, 1)
    return jnp.where(table < 0, -1, table - table[0:1] + lanes + HW).astype(F32)


def stage_kernel(
    frames_ref, cot_ref, table_ref, w_ref, frames_out, cot_out, table_out, w_out, picks_ref, sem
):
    pairs = (
        (table_ref, table_out),
        (w_ref, w_out),
        (frames_ref, frames_out),
        (cot_ref, cot_out),
    )
    moves = [pltpu.make_async_copy(a, b, sem.at[i]) for i, (a, b) in enumerate(pairs)]
    for move in moves:
        move.start()
    moves[0].wait()
    stencil, patch = table_out.shape
    places = slot_places(table_out[...])
    row = lax.broadcasted_iota(jnp.int32, (patch, patch), 0)
    square = jnp.full((patch, patch), -1.0, F32)
    for j in range(1, stencil):
        square = jnp.where(row == j, places[j : j + 1], square)
    columns = square.T
    lanes = lax.broadcasted_iota(jnp.int32, (patch, patch + 2 * HW), 1).astype(F32)
    for j in range(1, stencil):
        picks_ref[(j - 1) * patch : j * patch, :] = jnp.where(
            lanes == columns[:, j : j + 1], 1.0, 0.0
        ).astype(BF)
    for move in moves[1:]:
        move.wait()


def stage(frames, cotangent, table, w_conv):
    stencil, patch = table.shape
    return pl.pallas_call(
        stage_kernel,
        out_shape=(
            pltpu.VMEM(frames.shape, BF),
            pltpu.VMEM(cotangent.shape, BF),
            pltpu.VMEM(table.shape, jnp.int32),
            pltpu.VMEM(w_conv.shape, BF),
            pltpu.VMEM(((stencil - 1) * patch, patch + 2 * HW), BF),
        ),
        in_specs=[pl.BlockSpec(memory_space=pl.ANY)] * 4,
        scratch_shapes=[pltpu.SemaphoreType.DMA((4,))],
        name="stage",
        compiler_params=LIMIT,
    )(*(far_off(x) for x in (frames, cotangent, table, w_conv)))


def conv_forward_kernel(
    frames_ref, cot_ref, low_ref, high_ref, picks_ref, w_ref, sent_ref, pre_ref, gathered_ref
):
    frames_here, patch, width = frames_ref.shape
    stencil = picks_ref.shape[0] // patch + 1
    group = sent_ref.shape[3]
    for t in range(frames_here):
        rows = pl.ds(t * patch, patch)
        extended = jnp.concatenate([low_ref[t], frames_ref[t], high_ref[t]], axis=0)
        taken = mm(picks_ref[...], extended).astype(BF)
        gathered_ref[rows, 0:width] = frames_ref[t]
        for j in range(1, stencil):
            gathered_ref[rows, j * width : (j + 1) * width] = taken[(j - 1) * patch : j * patch]
        pre = mm(gathered_ref[rows, :], w_ref[...])
        pre_ref[rows, :] = pre
        gate = jax.nn.sigmoid(pre)
        hidden = (frames_ref[t].astype(F32) + pre * gate).astype(BF)
        for i in range(patch // group):
            sent_ref[i, 0, t] = hidden[i * group : (i + 1) * group]
            sent_ref[i, 1, t] = cot_ref[t, i * group : (i + 1) * group]


def conv_forward(frames, cotangent, low, high, picks, w_conv, parts):
    frames_here, patch, width = frames.shape
    rows = frames_here * patch
    return pl.pallas_call(
        conv_forward_kernel,
        out_shape=(
            pltpu.VMEM((parts, 2, frames_here, patch // parts, width), BF),
            pltpu.VMEM((rows, width), F32),
            pltpu.VMEM((rows, w_conv.shape[0]), BF),
        ),
        name="conv_forward",
        compiler_params=LIMIT,
    )(here(frames), here(cotangent), here(low), here(high), here(picks), here(w_conv))


def attention_kernel(came_ref, w_ref, back_ref, parts_ref):
    parts, _, frames_here, group, width = came_ref.shape
    frames_all = parts * frames_here
    rows_all = frames_all * group
    head_dim = width // HEADS
    scaling = head_dim ** (-0.5)
    half = 8
    rows = frames_all * half
    hidden = came_ref[:, 0].reshape(rows_all, width)
    grads = came_ref[:, 1].reshape(rows_all, width)

    def halves(values):
        cube = values.reshape(frames_all, group, width)
        return [cube[:, s : s + half].reshape(rows, width) for s in range(0, group, half)]

    query = halves(mm(hidden, w_ref[0]))
    key = halves(mm(hidden, w_ref[1]))
    value = halves(mm(hidden, w_ref[2]))
    grad_out = halves(mm_nt(grads, w_ref[3]))
    lane_head = lax.broadcasted_iota(jnp.int32, (rows, width), 1) // head_dim
    same = (
        lax.broadcasted_iota(jnp.int32, (rows, rows), 0) % half
        == lax.broadcasted_iota(jnp.int32, (rows, rows), 1) % half
    )
    same = jnp.where(same, 1.0, 0.0).astype(F32).reshape(1, frames_all, half, rows)

    def spread(values):
        return jnp.concatenate(
            [jnp.where(lane_head == h, values, 0.0).astype(BF) for h in range(HEADS)], axis=0
        )

    def collect(values):
        total = jnp.where(lane_head == 0, values[0:rows], 0.0)
        for h in range(1, HEADS):
            total = jnp.where(lane_head == h, values[h * rows : (h + 1) * rows], total)
        return total

    results = []
    for q32, k32, v32, g32 in zip(query, key, value, grad_out):
        q, g = q32.astype(BF), g32.astype(BF)
        k_heads, v_heads = spread(k32), spread(v32)
        shape4 = (HEADS, frames_all, half, rows)
        scores = mm_nt(k_heads, q).reshape(shape4) * scaling
        expo = jnp.exp(scores - jnp.max(scores, axis=1, keepdims=True))
        probs = expo * (same / jnp.sum(expo, axis=1, keepdims=True))
        probs_b = probs.reshape(-1, rows).astype(BF)
        grad_probs = mm_nt(v_heads, g).reshape(shape4)
        inner = jnp.sum(probs * grad_probs, axis=1, keepdims=True)
        grad_scores = (scaling * probs * (grad_probs - inner)).reshape(-1, rows).astype(BF)
        results.append(
            (
                mm_tn(probs_b, v_heads),
                mm_tn(grad_scores, k_heads),
                collect(mm(grad_scores, q)),
                collect(mm(probs_b, g)),
            )
        )

    def joined(index):
        pieces = [r[index].reshape(frames_all, half, width) for r in results]
        return jnp.concatenate(pieces, axis=1).reshape(rows_all, width).astype(BF)

    attended, grad_query, grad_key, grad_value = (joined(i) for i in range(4))
    back = (
        grads.astype(F32)
        + mm_nt(grad_query, w_ref[0])
        + mm_nt(grad_key, w_ref[1])
        + mm_nt(grad_value, w_ref[2])
    )
    back_ref[...] = back.astype(BF).reshape(back_ref.shape)
    parts_ref[0:width] = mm_tn(hidden, grad_query).astype(parts_ref.dtype)
    parts_ref[1 * width : 2 * width] = mm_tn(hidden, grad_key).astype(parts_ref.dtype)
    parts_ref[2 * width : 3 * width] = mm_tn(hidden, grad_value).astype(parts_ref.dtype)
    parts_ref[3 * width : 4 * width] = mm_tn(attended, grads).astype(parts_ref.dtype)


def attention(came, w_attn):
    parts, _, frames_here, group, width = came.shape
    return pl.pallas_call(
        attention_kernel,
        out_shape=(
            pltpu.VMEM((parts, frames_here, group, width), BF),
            pltpu.VMEM((4 * width, width), BF),
        ),
        name="attention",
        compiler_params=LIMIT,
    )(here(came), w_attn)


def conv_backward_kernel(
    back_ref,
    pre_ref,
    gathered_ref,
    table_ref,
    w_ref,
    attn_ref,
    local_ref,
    low_ref,
    high_ref,
    kept_ref,
    given_ref,
):
    parts, frames_here, group, width = back_ref.shape
    patch = parts * group
    stencil = table_ref.shape[0]
    places = slot_places(table_ref[...])
    target = lax.broadcasted_iota(jnp.int32, (patch + 2 * HW, patch), 0).astype(F32)
    puts = jnp.concatenate(
        [jnp.where(target == places[j : j + 1], 1.0, 0.0).astype(BF) for j in range(stencil)],
        axis=1,
    )
    pre = pre_ref[...]
    gate = jax.nn.sigmoid(pre)
    slope = gate * (1.0 + pre * (1.0 - gate))
    backs, grads = [], []
    for t in range(frames_here):
        back = jnp.concatenate([back_ref[i, t] for i in range(parts)], axis=0).astype(F32)
        backs.append(back)
        grads.append((back * slope[t * patch : (t + 1) * patch]).astype(BF))
    for t in range(frames_here):
        spread = mm_nt(grads[t], w_ref[...]).astype(BF)
        stacked = jnp.concatenate(
            [spread[:, j * width : (j + 1) * width] for j in range(stencil)], axis=0
        )
        extended = mm(puts, stacked)
        low_ref[t] = extended[0:HW].astype(low_ref.dtype)
        high_ref[t] = extended[patch + HW :].astype(high_ref.dtype)
        local_ref[t] = backs[t] + extended[HW : HW + patch]
    grad_pre = jnp.concatenate(grads, axis=0)
    grad_w = mm_tn(gathered_ref[...], grad_pre).astype(BF)
    near = kept_ref.shape[0]
    conv_rows = grad_w.shape[0] // (2 * near)
    attn_rows = attn_ref.shape[0] // (2 * near)
    first = lax.axis_index(PAIR) == 0
    for i in range(near):
        for source, rows, start in ((grad_w, conv_rows, 0), (attn_ref, attn_rows, conv_rows)):
            lower = source[i * rows : (i + 1) * rows]
            upper = source[(near + i) * rows : (near + i + 1) * rows]
            kept_ref[i, start : start + rows] = jnp.where(first, lower, upper)
            given_ref[i, start : start + rows] = jnp.where(first, upper, lower)


def conv_backward(back, pre, gathered, table, w_conv, attn_parts, near):
    parts, frames_here, group, width = back.shape
    patch = parts * group
    weight_rows = (w_conv.shape[0] + attn_parts.shape[0]) // (2 * near)
    return pl.pallas_call(
        conv_backward_kernel,
        out_shape=(
            pltpu.VMEM((frames_here, patch, width), F32),
            pltpu.VMEM((frames_here, HW, width), BF),
            pltpu.VMEM((frames_here, HW, width), BF),
            pltpu.VMEM((near, weight_rows, width), BF),
            pltpu.VMEM((near, weight_rows, width), BF),
        ),
        name="conv_backward",
        compiler_params=LIMIT,
    )(here(back), here(pre), here(gathered), here(table), here(w_conv), here(attn_parts))


LANES = 128


def pair_sum_kernel(kept_ref, came_ref, sum_ref):
    sum_ref[...] = (kept_ref[...].astype(F32) + came_ref[...].astype(F32)).astype(BF)


def pair_sum(kept, came):
    return pl.pallas_call(
        pair_sum_kernel,
        out_shape=pltpu.VMEM(kept.shape, BF),
        name="pair_sum",
        compiler_params=LIMIT,
    )(here(kept), here(came))


def first_sum_kernel(came_ref, tiles_ref):
    total = came_ref[0].astype(F32)
    for i in range(1, came_ref.shape[0]):
        total = total + came_ref[i].astype(F32)
    total = total.astype(BF)
    columns = total.shape[1] // LANES
    count = total.shape[0] // TILE * columns
    for n in range(count):
        row, lane = n // columns * TILE, n % columns * LANES
        tiles_ref[n] = total[row : row + TILE, lane : lane + LANES]
    rest = tiles_ref.shape[0] - count
    if rest:
        tiles_ref[count:] = jnp.zeros((rest, TILE, LANES), BF)


def first_sum(came, tiles):
    return pl.pallas_call(
        first_sum_kernel,
        out_shape=pltpu.VMEM((tiles, TILE, LANES), BF),
        name="first_sum",
        compiler_params=LIMIT,
    )(here(came))


def second_sum_kernel(scaling, came_ref, copies_ref):
    total = (jnp.sum(came_ref[...].astype(F32), axis=0) * scaling).astype(BF)
    for i in range(copies_ref.shape[0]):
        copies_ref[i] = total


def second_sum(came, scaling):
    return pl.pallas_call(
        functools.partial(second_sum_kernel, scaling),
        out_shape=pltpu.VMEM(came.shape, BF),
        name="second_sum",
        compiler_params=LIMIT,
    )(here(came))


def untile_kernel(tiles_ref, copies_ref):
    rows, width = copies_ref.shape[1:]
    columns = width // LANES
    for n in range(rows // TILE * columns):
        row, lane = n // columns * TILE, n % columns * LANES
        tile = tiles_ref[n]
        for i in range(copies_ref.shape[0]):
            copies_ref[i, row : row + TILE, lane : lane + LANES] = tile


def untile(tiles, shape):
    return pl.pallas_call(
        untile_kernel, out_shape=pltpu.VMEM(shape, BF), name="untile", compiler_params=LIMIT
    )(here(tiles))


def unpack_kernel(own_ref, other_ref, conv_ref, attn_ref, sem):
    conv_rows = conv_ref.shape[2]
    mine = lax.axis_index(PAIR)
    moves = []
    for n, (ref, half) in enumerate(((own_ref, mine), (other_ref, 1 - mine))):
        moves.append(
            pltpu.make_async_copy(ref.at[:, 0:conv_rows], conv_ref.at[half], sem.at[n, 0])
        )
        moves.append(
            pltpu.make_async_copy(ref.at[:, conv_rows:], attn_ref.at[half], sem.at[n, 1])
        )
    for move in moves:
        move.start()
    for move in moves:
        move.wait()


def unpack(own, other, conv_rows, attn_rows):
    near, _, width = own.shape
    return pl.pallas_call(
        unpack_kernel,
        out_shape=(
            jax.ShapeDtypeStruct((2, near, conv_rows // (2 * near), width), BF),
            jax.ShapeDtypeStruct((2, near, attn_rows // (2 * near), width), BF),
        ),
        in_specs=[pl.BlockSpec(memory_space=pltpu.VMEM)] * 2,
        out_specs=[pl.BlockSpec(memory_space=pl.ANY)] * 2,
        scratch_shapes=[pltpu.SemaphoreType.DMA((2, 2))],
        name="unpack",
        compiler_params=LIMIT,
    )(here(own), here(other))


def exchange(values, axis):
    return lax.all_to_all(values, axis, 0, 0, tiled=True)


def far_off(values):
    return pltpu.with_memory_space_constraint(values, pltpu.HBM)


def here(values):
    return pltpu.with_memory_space_constraint(values, pltpu.VMEM)


def to_neighbours(upward, downward):
    count = lax.axis_size(VERT)
    steps = [(i, i + 1) for i in range(count - 1)]
    from_below = lax.ppermute(upward, VERT, steps)
    from_above = lax.ppermute(downward, VERT, [(b, a) for a, b in steps])
    return from_below, from_above


def swap(values):
    return lax.ppermute(values, PAIR, [(0, 1), (1, 0)])


def body(frames, cotangent, table, w_conv, w_attn):
    _, patch, _ = frames.shape
    parts = lax.axis_size(TM)
    patches = lax.axis_size(VERT)
    near, far = lax.axis_size(NEAR), lax.axis_size(FAR)
    low, high = to_neighbours(frames[:, patch - HW :], frames[:, :HW])
    frames, cotangent, table, w_conv, picks = stage(frames, cotangent, table.T, w_conv)
    sent, pre, gathered = conv_forward(frames, cotangent, low, high, picks, w_conv, parts)
    back_time, attn_parts = attention(exchange(sent, TM), w_attn)
    back = exchange(back_time, TM)
    local, rim_low, rim_high, kept, given = conv_backward(
        back, pre, gathered, table, w_conv, attn_parts, near
    )
    came = swap(given)
    from_below, from_above = to_neighbours(rim_high, rim_low)
    weights = pair_sum(kept, came)
    arrived = jnp.concatenate([from_below, from_above], axis=1).astype(F32)
    grad_frames = (local + arrived).astype(BF)
    count = weights[0].size // (TILE * LANES)
    each = -(-count // far)
    came = exchange(weights, NEAR)
    tiles = first_sum(came, each * far)
    scaling = 1.0 / math.sqrt(TF * patch * patches)
    came = exchange(tiles, FAR).reshape(far, each, TILE, LANES)
    copies = second_sum(came, scaling).reshape(tiles.shape)
    copies = untile(exchange(copies, FAR), weights.shape)
    own = exchange(copies, NEAR)
    grad_conv, grad_attn = unpack(own, swap(own), w_conv.shape[0], attn_parts.shape[0])
    return grad_frames, grad_conv.reshape(w_conv.shape), grad_attn.reshape(w_attn.shape)


def solution(mesh):
    parts, patches = mesh.devices.shape
    sizes = (parts // 4, 2, 2, patches // 16, 2, 2, 2, 2)
    fine = jax.sharding.Mesh(mesh.devices.reshape(sizes), TM + VERT)
    return jax.shard_map(
        body,
        mesh=fine,
        in_specs=(P(TM, VERT, None), P(TM, VERT, None), P(VERT, None), P(), P()),
        out_specs=(P(TM, VERT, None), P(), P()),
        check_vma=False,
    )
```

profile of v0, /device:TPU:1, one launch (start us, length us, event | category | flops | bytes accessed | tf_op | source)
XLA Modules:
  0.0 142.3 jit_solution(15860486896645463916)
XLA Ops:
  0.6 0.9 fusion
  1.5 8.7 %collective-permute-start.1 = (bf16[2,64,256]{2,1,0:T(8,128)(2,1)S(1)}, bf16[2,64,256]{2,1,0:T(8,128)(2,1)S(1)}, u32[]{:S(2)}, u32[]{:S(2)}) collective-permute-start(bf16[2,64,256]{2,1,0:T(8,128)(2,1)S(1)} %get-tuple-element.37), channel_id=1, source_target_pairs={{1,0},{2,1},{3,2},{4,3},{5,4},{6,5},{7,6},{8,7},{9,8},{10,9},{11,1... | collective-permute-start | bytes 196616 | tf_op jit(solution)/shard_map/ppermute | solution.py:408
  10.3 1.9 %collective-permute-start = (bf16[2,64,256]{2,1,0:T(8,128)(2,1)S(1)}, bf16[2,64,256]{2,1,0:T(8,128)(2,1)S(1)}, u32[]{:S(2)}, u32[]{:S(2)}) collective-permute-start(bf16[2,64,256]{2,1,0:T(8,128)(2,1)S(1)} %get-tuple-element.38), channel_id=1, source_target_pairs={{0,1},{1,2},{2,3},{3,4},{4,5},{5,6},{6,7},{7,8},{8,9},{9,10},{10,1... | collective-permute-start | bytes 196616 | tf_op jit(solution)/shard_map/ppermute | solution.py:407
  12.2 1.3 stage.1
  13.5 0.7 conv_forward.1
  14.3 19.8 %all_to_all.30.came_ref = bf16[8,2,2,16,256]{4,3,2,1,0:T(8,128)(2,1)S(1)} all-to-all(bf16[8,2,2,16,256]{4,3,2,1,0:T(8,128)(2,1)S(1)} %get-tuple-element.24), channel_id=1, replica_groups=mesh['x_hi'=2,'x_lo'=2,'z_hi'=2,'y_hi'=4,'y_lo'=2,'z_mid'=2,'z_lo'=2,'co..., dimensions={0} | all-to-all | bytes 524288 | tf_op jit(solution)/shard_map/all_to_all | solution.py:393
  34.1 2.3 %attention.1 = (bf16[8,2,16,256]{3,2,1,0:T(8,128)(2,1)S(1)}, bf16[1024,256]{1,0:T(8,128)(2,1)S(1)}) custom-call(bf16[8,2,2,16,256]{4,3,2,1,0:T(8,128)(2,1)S(1)} %all_to_all.30.came_ref, bf16[4,256,256]{2,1,0:T(8,128)(2,1)S(1)} %copy-done), custom_call_target="tpu_custom_call" | custom-call | tf_op jit(solution)/shard_map/attention/pallas_call | solution.py:206
  36.3 12.3 %all_to_all.31.back_ref = bf16[8,2,16,256]{3,2,1,0:T(8,128)(2,1)S(1)} all-to-all(bf16[8,2,16,256]{3,2,1,0:T(8,128)(2,1)S(1)} %get-tuple-element.25), channel_id=1, replica_groups=mesh['x_hi'=2,'x_lo'=2,'z_hi'=2,'y_hi'=4,'y_lo'=2,'z_mid'=2,'z_lo'=2,'co..., dimensions={0} | all-to-all | bytes 262144 | tf_op jit(solution)/shard_map/all_to_all | solution.py:393
  48.6 1.2 conv_backward.1
  49.9 3.9 %collective-permute-start.4 = (bf16[8,176,256]{2,1,0:T(8,128)(2,1)S(1)}, bf16[8,176,256]{2,1,0:T(8,128)(2,1)S(1)}, u32[]{:S(2)}, u32[]{:S(2)}) collective-permute-start(bf16[8,176,256]{2,1,0:T(8,128)(2,1)S(1)} %get-tuple-element.34), channel_id=1, source_target_pairs={{0,1},{1,0},{2,3},{3,2},{4,5},{5,4},{6,7},{7,6},{8,9},{9,8},{10,11... | collective-permute-start | bytes 2162696 | tf_op jit(solution)/shard_map/ppermute | solution.py:413
  53.8 1.8 %collective-permute-done.4.came_ref = bf16[8,176,256]{2,1,0:T(8,128)(2,1)S(1)} collective-permute-done((bf16[8,176,256]{2,1,0:T(8,128)(2,1)S(1)}, bf16[8,176,256]{2,1,0:T(8,128)(2,1)S(1)}, u32[]{:S(2)}, u32[]{:S(2)}) %collective-permute-start.4) | collective-permute-done | bytes 720928 | tf_op jit(solution)/shard_map/ppermute | solution.py:413
  55.6 0.2 pair_sum.1
  55.7 20.3 %all_to_all.32.came_ref = bf16[8,176,256]{2,1,0:T(8,128)(2,1)S(1)} all-to-all(bf16[8,176,256]{2,1,0:T(8,128)(2,1)S(1)} %pair_sum.1), channel_id=1, replica_groups=mesh['x_hi'=2,'x_lo'=2,'z_hi'=2,'y_hi'=4,'y_lo'=2,'z_mid'=2,'z_lo'=2,'co..., dimensions={0} | all-to-all | bytes 1441792 | tf_op jit(solution)/shard_map/all_to_all | solution.py:393
  76.0 0.1 first_sum.1
  76.1 21.9 %all_to_all.33 = bf16[32,16,128]{2,1,0:T(8,128)(2,1)S(1)} all-to-all(bf16[32,16,128]{2,1,0:T(8,128)(2,1)S(1)} %first_sum.1), channel_id=1, replica_groups=mesh['x_hi'=2,'x_lo'=2,'z_hi'=2,'y_hi'=4,'y_lo'=2,'z_mid'=2,'z_lo'=2,'co..., dimensions={0} | all-to-all | bytes 262144 | tf_op jit(solution)/shard_map/all_to_all | solution.py:393
  98.1 16.7 %all_to_all.34.tiles_ref = bf16[32,16,128]{2,1,0:T(8,128)(2,1)S(1)} all-to-all(bf16[32,16,128]{2,1,0:T(8,128)(2,1)S(1)} %bitcast.6), channel_id=1, replica_groups=mesh['x_hi'=2,'x_lo'=2,'z_hi'=2,'y_hi'=4,'y_lo'=2,'z_mid'=2,'z_lo'=2,'co..., dimensions={0} | all-to-all | bytes 262144 | tf_op jit(solution)/shard_map/all_to_all | solution.py:393
  114.8 0.1 untile.1
  114.9 11.8 %all_to_all.35.own_ref = bf16[8,176,256]{2,1,0:T(8,128)(2,1)S(1)} all-to-all(bf16[8,176,256]{2,1,0:T(8,128)(2,1)S(1)} %untile.1), channel_id=1, replica_groups=mesh['x_hi'=2,'x_lo'=2,'z_hi'=2,'y_hi'=4,'y_lo'=2,'z_mid'=2,'z_lo'=2,'co..., dimensions={0} | all-to-all | bytes 1441792 | tf_op jit(solution)/shard_map/all_to_all | solution.py:393
  126.7 6.3 %collective-permute-start.5 = (bf16[8,176,256]{2,1,0:T(8,128)(2,1)S(1)}, bf16[8,176,256]{2,1,0:T(8,128)(2,1)S(1)}, u32[]{:S(2)}, u32[]{:S(2)}) collective-permute-start(bf16[8,176,256]{2,1,0:T(8,128)(2,1)S(1)} %all_to_all.35.own_ref), channel_id=1, source_target_pairs={{0,1},{1,0},{2,3},{3,2},{4,5},{5,4},{6,7},{7,6},{8,9},{9,8},{10,11... | collective-permute-start | bytes 2162696 | tf_op jit(solution)/shard_map/ppermute | solution.py:413
  133.0 1.9 %collective-permute-start.2 = (bf16[2,64,256]{2,1,0:T(8,128)(2,1)S(1)}, bf16[2,64,256]{2,1,0:T(8,128)(2,1)S(1)}, u32[]{:S(2)}, u32[]{:S(2)}) collective-permute-start(bf16[2,64,256]{2,1,0:T(8,128)(2,1)S(1)} %get-tuple-element.31), channel_id=1, source_target_pairs={{0,1},{1,2},{2,3},{3,4},{4,5},{5,6},{6,7},{7,8},{8,9},{9,10},{10,1... | collective-permute-start | bytes 196616 | tf_op jit(solution)/shard_map/ppermute | solution.py:407
  134.9 2.4 %collective-permute-start.3 = (bf16[2,64,256]{2,1,0:T(8,128)(2,1)S(1)}, bf16[2,64,256]{2,1,0:T(8,128)(2,1)S(1)}, u32[]{:S(2)}, u32[]{:S(2)}) collective-permute-start(bf16[2,64,256]{2,1,0:T(8,128)(2,1)S(1)} %get-tuple-element.32), channel_id=1, source_target_pairs={{1,0},{2,1},{3,2},{4,3},{5,4},{6,5},{7,6},{8,7},{9,8},{10,9},{11,1... | collective-permute-start | bytes 196616 | tf_op jit(solution)/shard_map/ppermute | solution.py:408
  137.3 3.2 %collective-permute-done.3 = bf16[2,64,256]{2,1,0:T(8,128)(2,1)S(1)} collective-permute-done((bf16[2,64,256]{2,1,0:T(8,128)(2,1)S(1)}, bf16[2,64,256]{2,1,0:T(8,128)(2,1)S(1)}, u32[]{:S(2)}, u32[]{:S(2)}) %collective-permute-start.3) | collective-permute-done | bytes 65568 | tf_op jit(solution)/shard_map/ppermute | solution.py:408
  140.5 0.7 add_convert_fusion
  141.2 1.1 unpack.1
  (7 shorter events, 0.1 us)
Async XLA Ops:
  1.5 12.0 %collective-permute-start.1 = (bf16[2,64,256]{2,1,0:T(8,128)(2,1)S(1)}, bf16[2,64,256]{2,1,0:T(8,128)(2,1)S(1)}, u32[]{:S(2)}, u32[]{:S(2)}) collective-permute-start(bf16[2,64,256]{2,1,0:T(8,128)(2,1)S(1)} %get-tuple-element.37), channel_id=1, source_target_pairs={{1,0},{2,1},{3,2},{4,3},{5,4},{6,5},{7,6},{8,7},{9,8},{10,9},{11,1... | collective-permute-start | bytes 196616 | tf_op jit(solution)/shard_map/ppermute | solution.py:408
  10.3 3.2 %collective-permute-start = (bf16[2,64,256]{2,1,0:T(8,128)(2,1)S(1)}, bf16[2,64,256]{2,1,0:T(8,128)(2,1)S(1)}, u32[]{:S(2)}, u32[]{:S(2)}) collective-permute-start(bf16[2,64,256]{2,1,0:T(8,128)(2,1)S(1)} %get-tuple-element.38), channel_id=1, source_target_pairs={{0,1},{1,2},{2,3},{3,4},{4,5},{5,6},{6,7},{7,8},{8,9},{9,10},{10,1... | collective-permute-start | bytes 196616 | tf_op jit(solution)/shard_map/ppermute | solution.py:407
  14.2 19.8 %copy-start = (bf16[4,256,256]{2,1,0:T(8,128)(2,1)S(1)}, bf16[4,256,256]{2,1,0:T(8,128)(2,1)}, u32[]{:S(2)}) copy-start(bf16[4,256,256]{2,1,0:T(8,128)(2,1)} %w_ref.3) | copy-start | bytes 1572868
  49.9 5.7 %collective-permute-start.4 = (bf16[8,176,256]{2,1,0:T(8,128)(2,1)S(1)}, bf16[8,176,256]{2,1,0:T(8,128)(2,1)S(1)}, u32[]{:S(2)}, u32[]{:S(2)}) collective-permute-start(bf16[8,176,256]{2,1,0:T(8,128)(2,1)S(1)} %get-tuple-element.34), channel_id=1, source_target_pairs={{0,1},{1,0},{2,3},{3,2},{4,5},{5,4},{6,7},{7,6},{8,9},{9,8},{10,11... | collective-permute-start | bytes 2162696 | tf_op jit(solution)/shard_map/ppermute | solution.py:413
  126.7 14.5 %collective-permute-start.5 = (bf16[8,176,256]{2,1,0:T(8,128)(2,1)S(1)}, bf16[8,176,256]{2,1,0:T(8,128)(2,1)S(1)}, u32[]{:S(2)}, u32[]{:S(2)}) collective-permute-start(bf16[8,176,256]{2,1,0:T(8,128)(2,1)S(1)} %all_to_all.35.own_ref), channel_id=1, source_target_pairs={{0,1},{1,0},{2,3},{3,2},{4,5},{5,4},{6,7},{7,6},{8,9},{9,8},{10,11... | collective-permute-start | bytes 2162696 | tf_op jit(solution)/shard_map/ppermute | solution.py:413
  133.0 4.3 %collective-permute-start.2 = (bf16[2,64,256]{2,1,0:T(8,128)(2,1)S(1)}, bf16[2,64,256]{2,1,0:T(8,128)(2,1)S(1)}, u32[]{:S(2)}, u32[]{:S(2)}) collective-permute-start(bf16[2,64,256]{2,1,0:T(8,128)(2,1)S(1)} %get-tuple-element.31), channel_id=1, source_target_pairs={{0,1},{1,2},{2,3},{3,4},{4,5},{5,6},{6,7},{7,8},{8,9},{9,10},{10,1... | collective-permute-start | bytes 196616 | tf_op jit(solution)/shard_map/ppermute | solution.py:407
  134.9 5.6 %collective-permute-start.3 = (bf16[2,64,256]{2,1,0:T(8,128)(2,1)S(1)}, bf16[2,64,256]{2,1,0:T(8,128)(2,1)S(1)}, u32[]{:S(2)}, u32[]{:S(2)}) collective-permute-start(bf16[2,64,256]{2,1,0:T(8,128)(2,1)S(1)} %get-tuple-element.32), channel_id=1, source_target_pairs={{1,0},{2,1},{3,2},{4,3},{5,4},{6,5},{7,6},{8,7},{9,8},{10,9},{11,1... | collective-permute-start | bytes 196616 | tf_op jit(solution)/shard_map/ppermute | solution.py:408
where the time goes:
time: 143 us; the launch traced here: 142 us
  blocking collectives  103 us (72%)
  starting transfers between devices  25.2 us (18%)
  Pallas kernels  7.01 us (5%)
  waiting for transfers between devices  4.98 us (3%)
    all_to_all x6, blocking collectives, exchange(): return lax.all_to_all(values, axis, 0, 0, tiled=True)  103 us
    ppermute x2, starting transfers between devices, to_neighbours(): from_above = lax.ppermute(downward, VERT, [(b, a) for a, b in steps])  11.2 us
    ppermute x2, starting transfers between devices, swap(): return lax.ppermute(values, PAIR, [(0, 1), (1, 0)])  10.2 us
    ppermute x2, starting transfers between devices, to_neighbours(): from_below = lax.ppermute(upward, VERT, steps)  3.84 us
    ppermute x2, waiting for transfers between devices, to_neighbours(): from_above = lax.ppermute(downward, VERT, [(b, a) for a, b in steps])  3.16 us
  transfers between devices with their start and end apart: 6, of which 2 were waited for; matrix products, arithmetic and copies ran while one was open for 0% of the time, Pallas kernels for 1%

commit v1 on v0

--- a/solution.py
+++ b/solution.py
@@ -1,4 +1,5 @@
 import functools
+import itertools
 import math
 
 import jax
@@ -393,6 +394,32 @@
     return lax.all_to_all(values, axis, 0, 0, tiled=True)
 
 
+def near_groups():
+    x_hi, x_lo, z_hi, y_hi, y_lo, z_mid, z_lo, cores = (lax.axis_size(a) for a in TM + VERT)
+    ends = (x_hi * x_lo, y_hi * y_lo, z_hi * z_mid * z_lo)
+    steps = (x_lo, y_lo, z_lo)
+    groups = []
+    for core in range(cores):
+        for corner in itertools.product(*(range(0, e, s) for e, s in zip(ends, steps))):
+            group = []
+            for parity in itertools.product(*(range(s) for s in steps)):
+                x, y, z = (
+                    (c + p + (core * s if p == 0 else 0)) % e
+                    for c, p, s, e in zip(corner, parity, steps, ends)
+                )
+                z_far, z_near = divmod(z, z_mid * z_lo)
+                place = ((x * z_hi + z_far) * ends[1] + y) * z_mid * z_lo + z_near
+                group.append(place * cores + core)
+            groups.append(group)
+    return groups
+
+
+def near_exchange(values):
+    return lax.all_to_all(
+        values, TM + VERT, 0, 0, axis_index_groups=near_groups(), tiled=True
+    )
+
+
 def far_off(values):
     return pltpu.with_memory_space_constraint(values, pltpu.HBM)
 
@@ -433,13 +460,13 @@
     grad_frames = (local + arrived).astype(BF)
     count = weights[0].size // (TILE * LANES)
     each = -(-count // far)
-    came = exchange(weights, NEAR)
+    came = near_exchange(weights)
     tiles = first_sum(came, each * far)
     scaling = 1.0 / math.sqrt(TF * patch * patches)
     came = exchange(tiles, FAR).reshape(far, each, TILE, LANES)
     copies = second_sum(came, scaling).reshape(tiles.shape)
     copies = untile(exchange(copies, FAR), weights.shape)
-    own = exchange(copies, NEAR)
+    own = near_exchange(copies)
     grad_conv, grad_attn = unpack(own, swap(own), w_conv.shape[0], attn_parts.shape[0])
     return grad_frames, grad_conv.reshape(w_conv.shape), grad_attn.reshape(w_attn.shape)
 

time: 143 us -> 142 us (level)
  starting transfers between devices: 25.2 us -> 20.8 us
  blocking collectives: 103 us -> 106 us
    all_to_all x0 -> x2, blocking collectives: none -> 37.9 us  [near_exchange(): lax.all_to_all(values, TM + VERT, 0, 0, axis_index_groups=near_groups(),...]
    all_to_all x6 -> x4, blocking collectives: 103 us -> 68.3 us  [exchange(): return lax.all_to_all(values, axis, 0, 0, tiled=True)]
    ppermute x2, starting transfers between devices: 10.2 us -> 5.8 us  [swap(): return lax.ppermute(values, PAIR, [(0, 1), (1, 0)])]
where the time goes in v1:
time: 142 us; the launch traced here: 141 us
  blocking collectives  106 us (75%)
  starting transfers between devices  20.8 us (15%)
  Pallas kernels  7.01 us (5%)
  waiting for transfers between devices  4.98 us (4%)
    all_to_all x4, blocking collectives, exchange(): return lax.all_to_all(values, axis, 0, 0, tiled=True)  68.3 us
    all_to_all x2, blocking collectives, near_exchange(): lax.all_to_all(values, TM + VERT, 0, 0, axis_index_groups=near_groups(),...  37.9 us
    ppermute x2, starting transfers between devices, to_neighbours(): from_above = lax.ppermute(downward, VERT, [(b, a) for a, b in steps])  11.2 us
    ppermute x2, starting transfers between devices, swap(): return lax.ppermute(values, PAIR, [(0, 1), (1, 0)])  5.8 us
    ppermute x2, starting transfers between devices, to_neighbours(): from_below = lax.ppermute(upward, VERT, steps)  3.84 us
    ppermute x2, waiting for transfers between devices, to_neighbours(): from_above = lax.ppermute(downward, VERT, [(b, a) for a, b in steps])  3.16 us
  transfers between devices with their start and end apart: 6, of which 2 were waited for; matrix products, arithmetic and copies ran while one was open for 0% of the time, Pallas kernels for 1%

profile of v1, /device:TPU:1, one launch (start us, length us, event | category | flops | bytes accessed | tf_op | source)
XLA Modules:
  0.0 141.4 jit_solution(1588906536448277462)
XLA Ops:
  0.6 0.9 fusion
  1.5 8.7 %collective-permute-start.1 = (bf16[2,64,256]{2,1,0:T(8,128)(2,1)S(1)}, bf16[2,64,256]{2,1,0:T(8,128)(2,1)S(1)}, u32[]{:S(2)}, u32[]{:S(2)}) collective-permute-start(bf16[2,64,256]{2,1,0:T(8,128)(2,1)S(1)} %get-tuple-element.37), channel_id=1, source_target_pairs={{1,0},{2,1},{3,2},{4,3},{5,4},{6,5},{7,6},{8,7},{9,8},{10,9},{11,1... | collective-permute-start | bytes 196616 | tf_op jit(solution)/shard_map/ppermute | solution.py:435
  10.3 1.9 %collective-permute-start = (bf16[2,64,256]{2,1,0:T(8,128)(2,1)S(1)}, bf16[2,64,256]{2,1,0:T(8,128)(2,1)S(1)}, u32[]{:S(2)}, u32[]{:S(2)}) collective-permute-start(bf16[2,64,256]{2,1,0:T(8,128)(2,1)S(1)} %get-tuple-element.38), channel_id=1, source_target_pairs={{0,1},{1,2},{2,3},{3,4},{4,5},{5,6},{6,7},{7,8},{8,9},{9,10},{10,1... | collective-permute-start | bytes 196616 | tf_op jit(solution)/shard_map/ppermute | solution.py:434
  12.2 1.3 stage.1
  13.5 0.7 conv_forward.1
  14.3 19.8 %all_to_all.30.came_ref = bf16[8,2,2,16,256]{4,3,2,1,0:T(8,128)(2,1)S(1)} all-to-all(bf16[8,2,2,16,256]{4,3,2,1,0:T(8,128)(2,1)S(1)} %get-tuple-element.24), channel_id=1, replica_groups=mesh['x_hi'=2,'x_lo'=2,'z_hi'=2,'y_hi'=4,'y_lo'=2,'z_mid'=2,'z_lo'=2,'co..., dimensions={0} | all-to-all | bytes 524288 | tf_op jit(solution)/shard_map/all_to_all | solution.py:394
  34.1 2.3 %attention.1 = (bf16[8,2,16,256]{3,2,1,0:T(8,128)(2,1)S(1)}, bf16[1024,256]{1,0:T(8,128)(2,1)S(1)}) custom-call(bf16[8,2,2,16,256]{4,3,2,1,0:T(8,128)(2,1)S(1)} %all_to_all.30.came_ref, bf16[4,256,256]{2,1,0:T(8,128)(2,1)S(1)} %copy-done), custom_call_target="tpu_custom_call" | custom-call | tf_op jit(solution)/shard_map/attention/pallas_call | solution.py:207
  36.3 12.3 %all_to_all.31.back_ref = bf16[8,2,16,256]{3,2,1,0:T(8,128)(2,1)S(1)} all-to-all(bf16[8,2,16,256]{3,2,1,0:T(8,128)(2,1)S(1)} %get-tuple-element.25), channel_id=1, replica_groups=mesh['x_hi'=2,'x_lo'=2,'z_hi'=2,'y_hi'=4,'y_lo'=2,'z_mid'=2,'z_lo'=2,'co..., dimensions={0} | all-to-all | bytes 262144 | tf_op jit(solution)/shard_map/all_to_all | solution.py:394
  48.6 1.2 conv_backward.1
  49.9 3.9 %collective-permute-start.4 = (bf16[8,176,256]{2,1,0:T(8,128)(2,1)S(1)}, bf16[8,176,256]{2,1,0:T(8,128)(2,1)S(1)}, u32[]{:S(2)}, u32[]{:S(2)}) collective-permute-start(bf16[8,176,256]{2,1,0:T(8,128)(2,1)S(1)} %get-tuple-element.34), channel_id=1, source_target_pairs={{0,1},{1,0},{2,3},{3,2},{4,5},{5,4},{6,7},{7,6},{8,9},{9,8},{10,11... | collective-permute-start | bytes 2162696 | tf_op jit(solution)/shard_map/ppermute | solution.py:440
  53.8 1.8 %collective-permute-done.4.came_ref = bf16[8,176,256]{2,1,0:T(8,128)(2,1)S(1)} collective-permute-done((bf16[8,176,256]{2,1,0:T(8,128)(2,1)S(1)}, bf16[8,176,256]{2,1,0:T(8,128)(2,1)S(1)}, u32[]{:S(2)}, u32[]{:S(2)}) %collective-permute-start.4) | collective-permute-done | bytes 720928 | tf_op jit(solution)/shard_map/ppermute | solution.py:440
  55.6 0.2 pair_sum.1
  55.7 23.6 %all_to_all.32.came_ref = bf16[8,176,256]{2,1,0:T(8,128)(2,1)S(1)} all-to-all(bf16[8,176,256]{2,1,0:T(8,128)(2,1)S(1)} %pair_sum.1), channel_id=1, replica_groups={{0,2,8,10,128,130,136,138},{4,6,12,14,132,134,140,142},{64,66,72,74,192..., dimensions={0} | all-to-all | bytes 1441792 | tf_op jit(solution)/shard_map/all_to_all | solution.py:418
  79.3 0.1 first_sum.1
  79.4 19.0 %all_to_all.33 = bf16[32,16,128]{2,1,0:T(8,128)(2,1)S(1)} all-to-all(bf16[32,16,128]{2,1,0:T(8,128)(2,1)S(1)} %first_sum.1), channel_id=1, replica_groups=mesh['x_hi'=2,'x_lo'=2,'z_hi'=2,'y_hi'=4,'y_lo'=2,'z_mid'=2,'z_lo'=2,'co..., dimensions={0} | all-to-all | bytes 262144 | tf_op jit(solution)/shard_map/all_to_all | solution.py:394
  98.5 17.2 %all_to_all.34.tiles_ref = bf16[32,16,128]{2,1,0:T(8,128)(2,1)S(1)} all-to-all(bf16[32,16,128]{2,1,0:T(8,128)(2,1)S(1)} %bitcast.6), channel_id=1, replica_groups=mesh['x_hi'=2,'x_lo'=2,'z_hi'=2,'y_hi'=4,'y_lo'=2,'z_mid'=2,'z_lo'=2,'co..., dimensions={0} | all-to-all | bytes 262144 | tf_op jit(solution)/shard_map/all_to_all | solution.py:394
  115.7 0.1 untile.1
  115.8 14.3 %all_to_all.35.own_ref = bf16[8,176,256]{2,1,0:T(8,128)(2,1)S(1)} all-to-all(bf16[8,176,256]{2,1,0:T(8,128)(2,1)S(1)} %untile.1), channel_id=1, replica_groups={{0,2,8,10,128,130,136,138},{4,6,12,14,132,134,140,142},{64,66,72,74,192..., dimensions={0} | all-to-all | bytes 1441792 | tf_op jit(solution)/shard_map/all_to_all | solution.py:418
  130.1 1.9 %collective-permute-start.5 = (bf16[8,176,256]{2,1,0:T(8,128)(2,1)S(1)}, bf16[8,176,256]{2,1,0:T(8,128)(2,1)S(1)}, u32[]{:S(2)}, u32[]{:S(2)}) collective-permute-start(bf16[8,176,256]{2,1,0:T(8,128)(2,1)S(1)} %all_to_all.35.own_ref), channel_id=1, source_target_pairs={{0,1},{1,0},{2,3},{3,2},{4,5},{5,4},{6,7},{7,6},{8,9},{9,8},{10,11... | collective-permute-start | bytes 2162696 | tf_op jit(solution)/shard_map/ppermute | solution.py:440
  132.0 1.9 %collective-permute-start.2 = (bf16[2,64,256]{2,1,0:T(8,128)(2,1)S(1)}, bf16[2,64,256]{2,1,0:T(8,128)(2,1)S(1)}, u32[]{:S(2)}, u32[]{:S(2)}) collective-permute-start(bf16[2,64,256]{2,1,0:T(8,128)(2,1)S(1)} %get-tuple-element.31), channel_id=1, source_target_pairs={{0,1},{1,2},{2,3},{3,4},{4,5},{5,6},{6,7},{7,8},{8,9},{9,10},{10,1... | collective-permute-start | bytes 196616 | tf_op jit(solution)/shard_map/ppermute | solution.py:434
  134.0 2.4 %collective-permute-start.3 = (bf16[2,64,256]{2,1,0:T(8,128)(2,1)S(1)}, bf16[2,64,256]{2,1,0:T(8,128)(2,1)S(1)}, u32[]{:S(2)}, u32[]{:S(2)}) collective-permute-start(bf16[2,64,256]{2,1,0:T(8,128)(2,1)S(1)} %get-tuple-element.32), channel_id=1, source_target_pairs={{1,0},{2,1},{3,2},{4,3},{5,4},{6,5},{7,6},{8,7},{9,8},{10,9},{11,1... | collective-permute-start | bytes 196616 | tf_op jit(solution)/shard_map/ppermute | solution.py:435
  136.4 3.2 %collective-permute-done.3 = bf16[2,64,256]{2,1,0:T(8,128)(2,1)S(1)} collective-permute-done((bf16[2,64,256]{2,1,0:T(8,128)(2,1)S(1)}, bf16[2,64,256]{2,1,0:T(8,128)(2,1)S(1)}, u32[]{:S(2)}, u32[]{:S(2)}) %collective-permute-start.3) | collective-permute-done | bytes 65568 | tf_op jit(solution)/shard_map/ppermute | solution.py:435
  139.5 0.7 add_convert_fusion
  140.2 1.1 unpack.1
  (7 shorter events, 0.1 us)
Async XLA Ops:
  1.5 12.0 %collective-permute-start.1 = (bf16[2,64,256]{2,1,0:T(8,128)(2,1)S(1)}, bf16[2,64,256]{2,1,0:T(8,128)(2,1)S(1)}, u32[]{:S(2)}, u32[]{:S(2)}) collective-permute-start(bf16[2,64,256]{2,1,0:T(8,128)(2,1)S(1)} %get-tuple-element.37), channel_id=1, source_target_pairs={{1,0},{2,1},{3,2},{4,3},{5,4},{6,5},{7,6},{8,7},{9,8},{10,9},{11,1... | collective-permute-start | bytes 196616 | tf_op jit(solution)/shard_map/ppermute | solution.py:435
  10.3 3.2 %collective-permute-start = (bf16[2,64,256]{2,1,0:T(8,128)(2,1)S(1)}, bf16[2,64,256]{2,1,0:T(8,128)(2,1)S(1)}, u32[]{:S(2)}, u32[]{:S(2)}) collective-permute-start(bf16[2,64,256]{2,1,0:T(8,128)(2,1)S(1)} %get-tuple-element.38), channel_id=1, source_target_pairs={{0,1},{1,2},{2,3},{3,4},{4,5},{5,6},{6,7},{7,8},{8,9},{9,10},{10,1... | collective-permute-start | bytes 196616 | tf_op jit(solution)/shard_map/ppermute | solution.py:434
  14.2 19.8 %copy-start = (bf16[4,256,256]{2,1,0:T(8,128)(2,1)S(1)}, bf16[4,256,256]{2,1,0:T(8,128)(2,1)}, u32[]{:S(2)}) copy-start(bf16[4,256,256]{2,1,0:T(8,128)(2,1)} %w_ref.3) | copy-start | bytes 1572868
  49.9 5.7 %collective-permute-start.4 = (bf16[8,176,256]{2,1,0:T(8,128)(2,1)S(1)}, bf16[8,176,256]{2,1,0:T(8,128)(2,1)S(1)}, u32[]{:S(2)}, u32[]{:S(2)}) collective-permute-start(bf16[8,176,256]{2,1,0:T(8,128)(2,1)S(1)} %get-tuple-element.34), channel_id=1, source_target_pairs={{0,1},{1,0},{2,3},{3,2},{4,5},{5,4},{6,7},{7,6},{8,9},{9,8},{10,11... | collective-permute-start | bytes 2162696 | tf_op jit(solution)/shard_map/ppermute | solution.py:440
  130.1 10.1 %collective-permute-start.5 = (bf16[8,176,256]{2,1,0:T(8,128)(2,1)S(1)}, bf16[8,176,256]{2,1,0:T(8,128)(2,1)S(1)}, u32[]{:S(2)}, u32[]{:S(2)}) collective-permute-start(bf16[8,176,256]{2,1,0:T(8,128)(2,1)S(1)} %all_to_all.35.own_ref), channel_id=1, source_target_pairs={{0,1},{1,0},{2,3},{3,2},{4,5},{5,4},{6,7},{7,6},{8,9},{9,8},{10,11... | collective-permute-start | bytes 2162696 | tf_op jit(solution)/shard_map/ppermute | solution.py:440
  132.0 4.3 %collective-permute-start.2 = (bf16[2,64,256]{2,1,0:T(8,128)(2,1)S(1)}, bf16[2,64,256]{2,1,0:T(8,128)(2,1)S(1)}, u32[]{:S(2)}, u32[]{:S(2)}) collective-permute-start(bf16[2,64,256]{2,1,0:T(8,128)(2,1)S(1)} %get-tuple-element.31), channel_id=1, source_target_pairs={{0,1},{1,2},{2,3},{3,4},{4,5},{5,6},{6,7},{7,8},{8,9},{9,10},{10,1... | collective-permute-start | bytes 196616 | tf_op jit(solution)/shard_map/ppermute | solution.py:434
  134.0 5.6 %collective-permute-start.3 = (bf16[2,64,256]{2,1,0:T(8,128)(2,1)S(1)}, bf16[2,64,256]{2,1,0:T(8,128)(2,1)S(1)}, u32[]{:S(2)}, u32[]{:S(2)}) collective-permute-start(bf16[2,64,256]{2,1,0:T(8,128)(2,1)S(1)} %get-tuple-element.32), channel_id=1, source_target_pairs={{1,0},{2,1},{3,2},{4,3},{5,4},{6,5},{7,6},{8,7},{9,8},{10,9},{11,1... | collective-permute-start | bytes 196616 | tf_op jit(solution)/shard_map/ppermute | solution.py:435

commit v2 on v0

--- a/solution.py
+++ b/solution.py
@@ -16,7 +16,8 @@
 VERT = ("y_hi", "y_lo", "z_mid", "z_lo", "core")
 PAIR = "core"
 NEAR = ("x_lo", "y_lo", "z_lo")
-FAR = ("x_hi", "z_hi", "y_hi", "z_mid")
+LINE = ("z_hi", "z_mid")
+PLANE = ("x_hi", "y_hi")
 TILE = 16
 BF = jnp.bfloat16
 F32 = jnp.float32
@@ -89,14 +90,17 @@
 
 
 def conv_forward_kernel(
-    frames_ref, cot_ref, low_ref, high_ref, picks_ref, w_ref, sent_ref, pre_ref, gathered_ref
+    frames_ref, cot_ref, outer_ref, inner_ref, picks_ref, w_ref, sent_ref, pre_ref, gathered_ref
 ):
     frames_here, patch, width = frames_ref.shape
     stencil = picks_ref.shape[0] // patch + 1
     group = sent_ref.shape[3]
+    first = lax.axis_index(PAIR) == 0
     for t in range(frames_here):
         rows = pl.ds(t * patch, patch)
-        extended = jnp.concatenate([low_ref[t], frames_ref[t], high_ref[t]], axis=0)
+        low = jnp.where(first, outer_ref[t], inner_ref[t])
+        high = jnp.where(first, inner_ref[t], outer_ref[t])
+        extended = jnp.concatenate([low, frames_ref[t], high], axis=0)
         taken = mm(picks_ref[...], extended).astype(BF)
         gathered_ref[rows, 0:width] = frames_ref[t]
         for j in range(1, stencil):
@@ -110,7 +114,7 @@
             sent_ref[i, 1, t] = cot_ref[t, i * group : (i + 1) * group]
 
 
-def conv_forward(frames, cotangent, low, high, picks, w_conv, parts):
+def conv_forward(frames, cotangent, outer, inner, picks, w_conv, parts):
     frames_here, patch, width = frames.shape
     rows = frames_here * patch
     return pl.pallas_call(
@@ -122,7 +126,7 @@
         ),
         name="conv_forward",
         compiler_params=LIMIT,
-    )(here(frames), here(cotangent), here(low), here(high), here(picks), here(w_conv))
+    )(here(frames), here(cotangent), here(outer), here(inner), here(picks), here(w_conv))
 
 
 def attention_kernel(came_ref, w_ref, back_ref, parts_ref):
@@ -222,8 +226,8 @@
     w_ref,
     attn_ref,
     local_ref,
-    low_ref,
-    high_ref,
+    outer_ref,
+    inner_ref,
     kept_ref,
     given_ref,
 ):
@@ -239,6 +243,7 @@
     pre = pre_ref[...]
     gate = jax.nn.sigmoid(pre)
     slope = gate * (1.0 + pre * (1.0 - gate))
+    first = lax.axis_index(PAIR) == 0
     backs, grads = [], []
     for t in range(frames_here):
         back = jnp.concatenate([back_ref[i, t] for i in range(parts)], axis=0).astype(F32)
@@ -250,15 +255,15 @@
             [spread[:, j * width : (j + 1) * width] for j in range(stencil)], axis=0
         )
         extended = mm(puts, stacked)
-        low_ref[t] = extended[0:HW].astype(low_ref.dtype)
-        high_ref[t] = extended[patch + HW :].astype(high_ref.dtype)
+        low, high = extended[0:HW].astype(BF), extended[patch + HW :].astype(BF)
+        outer_ref[t] = jnp.where(first, low, high)
+        inner_ref[t] = jnp.where(first, high, low)
         local_ref[t] = backs[t] + extended[HW : HW + patch]
     grad_pre = jnp.concatenate(grads, axis=0)
     grad_w = mm_tn(gathered_ref[...], grad_pre).astype(BF)
     near = kept_ref.shape[0]
     conv_rows = grad_w.shape[0] // (2 * near)
     attn_rows = attn_ref.shape[0] // (2 * near)
-    first = lax.axis_index(PAIR) == 0
     for i in range(near):
         for source, rows, start in ((grad_w, conv_rows, 0), (attn_ref, attn_rows, conv_rows)):
             lower = source[i * rows : (i + 1) * rows]
@@ -325,17 +330,19 @@
     )(here(came))
 
 
-def second_sum_kernel(scaling, came_ref, copies_ref):
-    total = (jnp.sum(came_ref[...].astype(F32), axis=0) * scaling).astype(BF)
+def spread_sum_kernel(scaling, came_ref, copies_ref):
+    total = jnp.sum(came_ref[...].astype(F32), axis=0)
+    if scaling is not None:
+        total = total * scaling
+    total = total.astype(BF)
     for i in range(copies_ref.shape[0]):
         copies_ref[i] = total
 
 
-def second_sum(came, scaling):
-    return pl.pallas_call(
-        functools.partial(second_sum_kernel, scaling),
-        out_shape=pltpu.VMEM(came.shape, BF),
-        name="second_sum",
+def spread_sum(came, scaling, copies):
+    return pl.pallas_call(
+        functools.partial(spread_sum_kernel, scaling),
+        out_shape=pltpu.VMEM((copies, *came.shape[1:]), BF),
         compiler_params=LIMIT,
     )(here(came))
 
@@ -401,12 +408,12 @@
     return pltpu.with_memory_space_constraint(values, pltpu.VMEM)
 
 
-def to_neighbours(upward, downward):
+def patch_swaps(outer, inner):
     count = lax.axis_size(VERT)
-    steps = [(i, i + 1) for i in range(count - 1)]
-    from_below = lax.ppermute(upward, VERT, steps)
-    from_above = lax.ppermute(downward, VERT, [(b, a) for a, b in steps])
-    return from_below, from_above
+    steps = [(i, i + 1) for i in range(1, count - 1, 2)]
+    from_outer = lax.ppermute(outer, VERT, steps + [(b, a) for a, b in steps])
+    from_inner = swap(inner)
+    return from_outer, from_inner
 
 
 def swap(values):
@@ -417,28 +424,38 @@
     _, patch, _ = frames.shape
     parts = lax.axis_size(TM)
     patches = lax.axis_size(VERT)
-    near, far = lax.axis_size(NEAR), lax.axis_size(FAR)
-    low, high = to_neighbours(frames[:, patch - HW :], frames[:, :HW])
+    near = lax.axis_size(NEAR)
+    core = lax.axis_index(PAIR)
+    low, high = frames[:, :HW], frames[:, patch - HW :]
+    outer, inner = patch_swaps(
+        jnp.where(core == 0, low, high), jnp.where(core == 0, high, low)
+    )
     frames, cotangent, table, w_conv, picks = stage(frames, cotangent, table.T, w_conv)
-    sent, pre, gathered = conv_forward(frames, cotangent, low, high, picks, w_conv, parts)
+    sent, pre, gathered = conv_forward(
+        frames, cotangent, outer, inner, picks, w_conv, parts
+    )
     back_time, attn_parts = attention(exchange(sent, TM), w_attn)
     back = exchange(back_time, TM)
-    local, rim_low, rim_high, kept, given = conv_backward(
+    local, rim_outer, rim_inner, kept, given = conv_backward(
         back, pre, gathered, table, w_conv, attn_parts, near
     )
     came = swap(given)
-    from_below, from_above = to_neighbours(rim_high, rim_low)
+    outer, inner = patch_swaps(rim_outer, rim_inner)
     weights = pair_sum(kept, came)
-    arrived = jnp.concatenate([from_below, from_above], axis=1).astype(F32)
+    low, high = jnp.where(core == 0, outer, inner), jnp.where(core == 0, inner, outer)
+    arrived = jnp.concatenate([low, high], axis=1).astype(F32)
     grad_frames = (local + arrived).astype(BF)
     count = weights[0].size // (TILE * LANES)
-    each = -(-count // far)
+    line, plane = lax.axis_size(LINE), lax.axis_size(PLANE)
+    each = -(-count // line)
     came = exchange(weights, NEAR)
-    tiles = first_sum(came, each * far)
+    tiles = first_sum(came, each * line)
+    came = exchange(tiles, LINE).reshape(line, each, TILE, LANES)
+    copies = spread_sum(came, None, plane)
+    came = exchange(copies, PLANE)
     scaling = 1.0 / math.sqrt(TF * patch * patches)
-    came = exchange(tiles, FAR).reshape(far, each, TILE, LANES)
-    copies = second_sum(came, scaling).reshape(tiles.shape)
-    copies = untile(exchange(copies, FAR), weights.shape)
+    copies = spread_sum(came, scaling, line).reshape(tiles.shape)
+    copies = untile(exchange(copies, LINE), weights.shape)
     own = exchange(copies, NEAR)
     grad_conv, grad_attn = unpack(own, swap(own), w_conv.shape[0], attn_parts.shape[0])
     return grad_frames, grad_conv.reshape(w_conv.shape), grad_attn.reshape(w_attn.shape)

time: 143 us -> 139 us (0.972)
  blocking collectives: 103 us -> 96.7 us
    ppermute x4 -> x2, starting transfers between devices: 15 us -> 3.84 us  [patch_swaps(): from_outer = lax.ppermute(outer, VERT, steps + [(b, a) for a, b in steps])]
    ppermute x2 -> x4, starting transfers between devices: 10.2 us -> 20.9 us  [swap(): return lax.ppermute(values, PAIR, [(0, 1), (1, 0)])]
    all_to_all x6 -> x7, blocking collectives: 103 us -> 96.7 us  [exchange(): return lax.all_to_all(values, axis, 0, 0, tiled=True)]
    ppermute x4 -> x2, waiting for transfers between devices: 3.18 us -> 4.09 us  [patch_swaps(): from_outer = lax.ppermute(outer, VERT, steps + [(b, a) for a, b in steps])]
  transfers between devices with their start and end apart: 6 -> 6, of which waited for: 2 -> 3; matrix products, arithmetic and copies ran while one was open for 0% -> 1% of each run, Pallas kernels for 1% -> 1%
where the time goes in v2:
time: 139 us; the launch traced here: 137 us
  blocking collectives  96.7 us (70%)
  starting transfers between devices  24.7 us (18%)
  Pallas kernels  7.02 us (5%)
  waiting for transfers between devices  6.26 us (5%)
  other arithmetic  1.59 us (1%)
    all_to_all x7, blocking collectives, exchange(): return lax.all_to_all(values, axis, 0, 0, tiled=True)  96.7 us
    ppermute x4, starting transfers between devices, swap(): return lax.ppermute(values, PAIR, [(0, 1), (1, 0)])  20.9 us
    ppermute x2, waiting for transfers between devices, patch_swaps(): from_outer = lax.ppermute(outer, VERT, steps + [(b, a) for a, b in steps])  4.09 us
    ppermute x2, starting transfers between devices, patch_swaps(): from_outer = lax.ppermute(outer, VERT, steps + [(b, a) for a, b in steps])  3.84 us
  transfers between devices with their start and end apart: 6, of which 3 were waited for; matrix products, arithmetic and copies ran while one was open for 1% of the time, Pallas kernels for 1%

profile of v2, /device:TPU:1, one launch (start us, length us, event | category | flops | bytes accessed | tf_op | source)
XLA Modules:
  0.0 137.1 jit_solution(10198845391302779228)
XLA Ops:
  0.6 0.9 broadcast_select_fusion.2
  1.5 8.7 %collective-permute-start.1 = (bf16[2,64,256]{2,1,0:T(8,128)(2,1)S(1)}, bf16[2,64,256]{2,1,0:T(8,128)(2,1)S(1)}, u32[]{:S(2)}, u32[]{:S(2)}) collective-permute-start(bf16[2,64,256]{2,1,0:T(8,128)(2,1)S(1)} %get-tuple-element.39), channel_id=1, source_target_pairs={{0,1},{1,0},{2,3},{3,2},{4,5},{5,4},{6,7},{7,6},{8,9},{9,8},{10,11... | collective-permute-start | bytes 196616 | tf_op jit(solution)/shard_map/ppermute | solution.py:420
  10.3 1.9 %collective-permute-start = (bf16[2,64,256]{2,1,0:T(8,128)(2,1)S(1)}, bf16[2,64,256]{2,1,0:T(8,128)(2,1)S(1)}, u32[]{:S(2)}, u32[]{:S(2)}) collective-permute-start(bf16[2,64,256]{2,1,0:T(8,128)(2,1)S(1)} %get-tuple-element.40), channel_id=1, source_target_pairs={{1,2},{3,4},{5,6},{7,8},{9,10},{11,12},{13,14},{15,16},{17,18},{19... | collective-permute-start | bytes 196616 | tf_op jit(solution)/shard_map/ppermute | solution.py:414
  12.2 1.3 stage.1
  13.5 2.4 %collective-permute-done.outer_ref = bf16[2,64,256]{2,1,0:T(8,128)(2,1)S(1)} collective-permute-done((bf16[2,64,256]{2,1,0:T(8,128)(2,1)S(1)}, bf16[2,64,256]{2,1,0:T(8,128)(2,1)S(1)}, u32[]{:S(2)}, u32[]{:S(2)}) %collective-permute-start) | collective-permute-done | bytes 65568 | tf_op jit(solution)/shard_map/ppermute | solution.py:414
  15.9 0.7 conv_forward.1
  16.6 17.2 %all_to_all.35.came_ref = bf16[8,2,2,16,256]{4,3,2,1,0:T(8,128)(2,1)S(1)} all-to-all(bf16[8,2,2,16,256]{4,3,2,1,0:T(8,128)(2,1)S(1)} %get-tuple-element.24), channel_id=1, replica_groups=mesh['x_hi'=2,'x_lo'=2,'z_hi'=2,'y_hi'=4,'y_lo'=2,'z_mid'=2,'z_lo'=2,'co..., dimensions={0} | all-to-all | bytes 524288 | tf_op jit(solution)/shard_map/all_to_all | solution.py:400
  33.8 2.3 %attention.1 = (bf16[8,2,16,256]{3,2,1,0:T(8,128)(2,1)S(1)}, bf16[1024,256]{1,0:T(8,128)(2,1)S(1)}) custom-call(bf16[8,2,2,16,256]{4,3,2,1,0:T(8,128)(2,1)S(1)} %all_to_all.35.came_ref, bf16[4,256,256]{2,1,0:T(8,128)(2,1)S(1)} %copy-done), custom_call_target="tpu_custom_call" | custom-call | tf_op jit(solution)/shard_map/attention/pallas_call | solution.py:210
  36.1 12.3 %all_to_all.36.back_ref = bf16[8,2,16,256]{3,2,1,0:T(8,128)(2,1)S(1)} all-to-all(bf16[8,2,16,256]{3,2,1,0:T(8,128)(2,1)S(1)} %get-tuple-element.25), channel_id=1, replica_groups=mesh['x_hi'=2,'x_lo'=2,'z_hi'=2,'y_hi'=4,'y_lo'=2,'z_mid'=2,'z_lo'=2,'co..., dimensions={0} | all-to-all | bytes 262144 | tf_op jit(solution)/shard_map/all_to_all | solution.py:400
  48.4 1.2 conv_backward.1
  49.6 1.9 %collective-permute-start.4 = (bf16[8,176,256]{2,1,0:T(8,128)(2,1)S(1)}, bf16[8,176,256]{2,1,0:T(8,128)(2,1)S(1)}, u32[]{:S(2)}, u32[]{:S(2)}) collective-permute-start(bf16[8,176,256]{2,1,0:T(8,128)(2,1)S(1)} %get-tuple-element.34), channel_id=1, source_target_pairs={{0,1},{1,0},{2,3},{3,2},{4,5},{5,4},{6,7},{7,6},{8,9},{9,8},{10,11... | collective-permute-start | bytes 2162696 | tf_op jit(solution)/shard_map/ppermute | solution.py:420
  51.5 2.2 %collective-permute-done.4.came_ref = bf16[8,176,256]{2,1,0:T(8,128)(2,1)S(1)} collective-permute-done((bf16[8,176,256]{2,1,0:T(8,128)(2,1)S(1)}, bf16[8,176,256]{2,1,0:T(8,128)(2,1)S(1)}, u32[]{:S(2)}, u32[]{:S(2)}) %collective-permute-start.4) | collective-permute-done | bytes 720928 | tf_op jit(solution)/shard_map/ppermute | solution.py:420
  53.7 0.2 pair_sum.1
  53.9 18.9 %all_to_all.37.came_ref = bf16[8,176,256]{2,1,0:T(8,128)(2,1)S(1)} all-to-all(bf16[8,176,256]{2,1,0:T(8,128)(2,1)S(1)} %pair_sum.1), channel_id=1, replica_groups=mesh['x_hi'=2,'x_lo'=2,'z_hi'=2,'y_hi'=4,'y_lo'=2,'z_mid'=2,'z_lo'=2,'co..., dimensions={0} | all-to-all | bytes 1441792 | tf_op jit(solution)/shard_map/all_to_all | solution.py:400
  72.9 10.6 %all_to_all.38 = bf16[24,16,128]{2,1,0:T(8,128)(2,1)S(1)} all-to-all(bf16[24,16,128]{2,1,0:T(8,128)(2,1)S(1)} %first_sum.1), channel_id=1, replica_groups=mesh['x_hi'=2,'x_lo'=2,'z_hi'=2,'y_hi'=4,'y_lo'=2,'z_mid'=2,'z_lo'=2,'co..., dimensions={0} | all-to-all | bytes 196608 | tf_op jit(solution)/shard_map/all_to_all | solution.py:400
  83.6 16.6 %all_to_all.39.came_ref = bf16[8,6,16,128]{3,2,1,0:T(8,128)(2,1)S(1)} all-to-all(bf16[8,6,16,128]{3,2,1,0:T(8,128)(2,1)S(1)} %shard_map.76), channel_id=1, replica_groups=mesh['x_hi'=2,'x_lo'=2,'z_hi'=2,'y_hi'=4,'y_lo'=2,'z_mid'=2,'z_lo'=2,'co..., dimensions={0} | all-to-all | bytes 393216 | tf_op jit(solution)/shard_map/all_to_all | solution.py:400
  100.2 9.4 %all_to_all.40.tiles_ref = bf16[24,16,128]{2,1,0:T(8,128)(2,1)S(1)} all-to-all(bf16[24,16,128]{2,1,0:T(8,128)(2,1)S(1)} %bitcast.6), channel_id=1, replica_groups=mesh['x_hi'=2,'x_lo'=2,'z_hi'=2,'y_hi'=4,'y_lo'=2,'z_mid'=2,'z_lo'=2,'co..., dimensions={0} | all-to-all | bytes 196608 | tf_op jit(solution)/shard_map/all_to_all | solution.py:400
  109.7 11.6 %all_to_all.41.own_ref = bf16[8,176,256]{2,1,0:T(8,128)(2,1)S(1)} all-to-all(bf16[8,176,256]{2,1,0:T(8,128)(2,1)S(1)} %untile.1), channel_id=1, replica_groups=mesh['x_hi'=2,'x_lo'=2,'z_hi'=2,'y_hi'=4,'y_lo'=2,'z_mid'=2,'z_lo'=2,'co..., dimensions={0} | all-to-all | bytes 1441792 | tf_op jit(solution)/shard_map/all_to_all | solution.py:400
  121.3 8.3 %collective-permute-start.5 = (bf16[8,176,256]{2,1,0:T(8,128)(2,1)S(1)}, bf16[8,176,256]{2,1,0:T(8,128)(2,1)S(1)}, u32[]{:S(2)}, u32[]{:S(2)}) collective-permute-start(bf16[8,176,256]{2,1,0:T(8,128)(2,1)S(1)} %all_to_all.41.own_ref), channel_id=1, source_target_pairs={{0,1},{1,0},{2,3},{3,2},{4,5},{5,4},{6,7},{7,6},{8,9},{9,8},{10,11... | collective-permute-start | bytes 2162696 | tf_op jit(solution)/shard_map/ppermute | solution.py:420
  129.6 1.9 %collective-permute-start.2 = (bf16[2,64,256]{2,1,0:T(8,128)(2,1)S(1)}, bf16[2,64,256]{2,1,0:T(8,128)(2,1)S(1)}, u32[]{:S(2)}, u32[]{:S(2)}) collective-permute-start(bf16[2,64,256]{2,1,0:T(8,128)(2,1)S(1)} %get-tuple-element.31), channel_id=1, source_target_pairs={{1,2},{3,4},{5,6},{7,8},{9,10},{11,12},{13,14},{15,16},{17,18},{19... | collective-permute-start | bytes 196616 | tf_op jit(solution)/shard_map/ppermute | solution.py:414
  131.6 1.9 %collective-permute-start.3 = (bf16[2,64,256]{2,1,0:T(8,128)(2,1)S(1)}, bf16[2,64,256]{2,1,0:T(8,128)(2,1)S(1)}, u32[]{:S(2)}, u32[]{:S(2)}) collective-permute-start(bf16[2,64,256]{2,1,0:T(8,128)(2,1)S(1)} %get-tuple-element.32), channel_id=1, source_target_pairs={{0,1},{1,0},{2,3},{3,2},{4,5},{5,4},{6,7},{7,6},{8,9},{9,8},{10,11... | collective-permute-start | bytes 196616 | tf_op jit(solution)/shard_map/ppermute | solution.py:420
  133.5 1.7 %collective-permute-done.2 = bf16[2,64,256]{2,1,0:T(8,128)(2,1)S(1)} collective-permute-done((bf16[2,64,256]{2,1,0:T(8,128)(2,1)S(1)}, bf16[2,64,256]{2,1,0:T(8,128)(2,1)S(1)}, u32[]{:S(2)}, u32[]{:S(2)}) %collective-permute-start.2) | collective-permute-done | bytes 65568 | tf_op jit(solution)/shard_map/ppermute | solution.py:414
  135.3 0.7 add_convert_fusion
  135.9 1.1 unpack.1
  (10 shorter events, 0.3 us)
Async XLA Ops:
  1.5 12.0 %collective-permute-start.1 = (bf16[2,64,256]{2,1,0:T(8,128)(2,1)S(1)}, bf16[2,64,256]{2,1,0:T(8,128)(2,1)S(1)}, u32[]{:S(2)}, u32[]{:S(2)}) collective-permute-start(bf16[2,64,256]{2,1,0:T(8,128)(2,1)S(1)} %get-tuple-element.39), channel_id=1, source_target_pairs={{0,1},{1,0},{2,3},{3,2},{4,5},{5,4},{6,7},{7,6},{8,9},{9,8},{10,11... | collective-permute-start | bytes 196616 | tf_op jit(solution)/shard_map/ppermute | solution.py:420
  10.3 5.6 %collective-permute-start = (bf16[2,64,256]{2,1,0:T(8,128)(2,1)S(1)}, bf16[2,64,256]{2,1,0:T(8,128)(2,1)S(1)}, u32[]{:S(2)}, u32[]{:S(2)}) collective-permute-start(bf16[2,64,256]{2,1,0:T(8,128)(2,1)S(1)} %get-tuple-element.40), channel_id=1, source_target_pairs={{1,2},{3,4},{5,6},{7,8},{9,10},{11,12},{13,14},{15,16},{17,18},{19... | collective-permute-start | bytes 196616 | tf_op jit(solution)/shard_map/ppermute | solution.py:414
  16.6 17.2 %copy-start = (bf16[4,256,256]{2,1,0:T(8,128)(2,1)S(1)}, bf16[4,256,256]{2,1,0:T(8,128)(2,1)}, u32[]{:S(2)}) copy-start(bf16[4,256,256]{2,1,0:T(8,128)(2,1)} %w_ref.3) | copy-start | bytes 1572868
  49.6 4.1 %collective-permute-start.4 = (bf16[8,176,256]{2,1,0:T(8,128)(2,1)S(1)}, bf16[8,176,256]{2,1,0:T(8,128)(2,1)S(1)}, u32[]{:S(2)}, u32[]{:S(2)}) collective-permute-start(bf16[8,176,256]{2,1,0:T(8,128)(2,1)S(1)} %get-tuple-element.34), channel_id=1, source_target_pairs={{0,1},{1,0},{2,3},{3,2},{4,5},{5,4},{6,7},{7,6},{8,9},{9,8},{10,11... | collective-permute-start | bytes 2162696 | tf_op jit(solution)/shard_map/ppermute | solution.py:420
  121.3 14.6 %collective-permute-start.5 = (bf16[8,176,256]{2,1,0:T(8,128)(2,1)S(1)}, bf16[8,176,256]{2,1,0:T(8,128)(2,1)S(1)}, u32[]{:S(2)}, u32[]{:S(2)}) collective-permute-start(bf16[8,176,256]{2,1,0:T(8,128)(2,1)S(1)} %all_to_all.41.own_ref), channel_id=1, source_target_pairs={{0,1},{1,0},{2,3},{3,2},{4,5},{5,4},{6,7},{7,6},{8,9},{9,8},{10,11... | collective-permute-start | bytes 2162696 | tf_op jit(solution)/shard_map/ppermute | solution.py:420
  129.6 5.6 %collective-permute-start.2 = (bf16[2,64,256]{2,1,0:T(8,128)(2,1)S(1)}, bf16[2,64,256]{2,1,0:T(8,128)(2,1)S(1)}, u32[]{:S(2)}, u32[]{:S(2)}) collective-permute-start(bf16[2,64,256]{2,1,0:T(8,128)(2,1)S(1)} %get-tuple-element.31), channel_id=1, source_target_pairs={{1,2},{3,4},{5,6},{7,8},{9,10},{11,12},{13,14},{15,16},{17,18},{19... | collective-permute-start | bytes 196616 | tf_op jit(solution)/shard_map/ppermute | solution.py:414
  131.6 3.7 %collective-permute-start.3 = (bf16[2,64,256]{2,1,0:T(8,128)(2,1)S(1)}, bf16[2,64,256]{2,1,0:T(8,128)(2,1)S(1)}, u32[]{:S(2)}, u32[]{:S(2)}) collective-permute-start(bf16[2,64,256]{2,1,0:T(8,128)(2,1)S(1)} %get-tuple-element.32), channel_id=1, source_target_pairs={{0,1},{1,0},{2,3},{3,2},{4,5},{5,4},{6,7},{7,6},{8,9},{9,8},{10,11... | collective-permute-start | bytes 196616 | tf_op jit(solution)/shard_map/ppermute | solution.py:420

commit v3 on v2

--- a/solution.py
+++ b/solution.py
@@ -363,37 +363,56 @@
     )(here(tiles))
 
 
-def unpack_kernel(own_ref, other_ref, conv_ref, attn_ref, sem):
+def unpack_half(half_ref, conv_ref, attn_ref, half, sem):
     conv_rows = conv_ref.shape[2]
-    mine = lax.axis_index(PAIR)
-    moves = []
-    for n, (ref, half) in enumerate(((own_ref, mine), (other_ref, 1 - mine))):
-        moves.append(
-            pltpu.make_async_copy(ref.at[:, 0:conv_rows], conv_ref.at[half], sem.at[n, 0])
-        )
-        moves.append(
-            pltpu.make_async_copy(ref.at[:, conv_rows:], attn_ref.at[half], sem.at[n, 1])
-        )
+    moves = [
+        pltpu.make_async_copy(half_ref.at[:, 0:conv_rows], conv_ref.at[half], sem.at[0]),
+        pltpu.make_async_copy(half_ref.at[:, conv_rows:], attn_ref.at[half], sem.at[1]),
+    ]
     for move in moves:
         move.start()
     for move in moves:
         move.wait()
 
 
-def unpack(own, other, conv_rows, attn_rows):
+def unpack_own_kernel(own_ref, conv_ref, attn_ref, sem):
+    unpack_half(own_ref, conv_ref, attn_ref, lax.axis_index(PAIR), sem)
+
+
+def unpack_other_kernel(other_ref, conv_in, attn_in, conv_ref, attn_ref, sem):
+    unpack_half(other_ref, conv_ref, attn_ref, 1 - lax.axis_index(PAIR), sem)
+
+
+def unpack_own(own, conv_rows, attn_rows):
     near, _, width = own.shape
     return pl.pallas_call(
-        unpack_kernel,
+        unpack_own_kernel,
         out_shape=(
             jax.ShapeDtypeStruct((2, near, conv_rows // (2 * near), width), BF),
             jax.ShapeDtypeStruct((2, near, attn_rows // (2 * near), width), BF),
         ),
-        in_specs=[pl.BlockSpec(memory_space=pltpu.VMEM)] * 2,
+        in_specs=[pl.BlockSpec(memory_space=pltpu.VMEM)],
         out_specs=[pl.BlockSpec(memory_space=pl.ANY)] * 2,
-        scratch_shapes=[pltpu.SemaphoreType.DMA((2, 2))],
-        name="unpack",
-        compiler_params=LIMIT,
-    )(here(own), here(other))
+        scratch_shapes=[pltpu.SemaphoreType.DMA((2,))],
+        name="unpack_own",
+        compiler_params=LIMIT,
+    )(here(own))
+
+
+def unpack_other(other, conv, attn):
+    return pl.pallas_call(
+        unpack_other_kernel,
+        out_shape=(
+            jax.ShapeDtypeStruct(conv.shape, BF),
+            jax.ShapeDtypeStruct(attn.shape, BF),
+        ),
+        in_specs=[pl.BlockSpec(memory_space=pltpu.VMEM)] + [pl.BlockSpec(memory_space=pl.ANY)] * 2,
+        out_specs=[pl.BlockSpec(memory_space=pl.ANY)] * 2,
+        scratch_shapes=[pltpu.SemaphoreType.DMA((2,))],
+        input_output_aliases={1: 0, 2: 1},
+        name="unpack_other",
+        compiler_params=LIMIT,
+    )(here(other), conv, attn)
 
 
 def exchange(values, axis):
@@ -457,7 +476,10 @@
     copies = spread_sum(came, scaling, line).reshape(tiles.shape)
     copies = untile(exchange(copies, LINE), weights.shape)
     own = exchange(copies, NEAR)
-    grad_conv, grad_attn = unpack(own, swap(own), w_conv.shape[0], attn_parts.shape[0])
+    other = swap(own)
+    grad_conv, grad_attn = unpack_other(
+        other, *unpack_own(own, w_conv.shape[0], attn_parts.shape[0])
+    )
     return grad_frames, grad_conv.reshape(w_conv.shape), grad_attn.reshape(w_attn.shape)
 
 

time: 139 us -> 139 us (level)
  transfers between devices with their start and end apart: 6 -> 6, of which waited for: 3 -> 3; matrix products, arithmetic and copies ran while one was open for 1% -> 1% of each run, Pallas kernels for 1% -> 2%
where the time goes in v3:
time: 139 us; the launch traced here: 138 us
  blocking collectives  96.7 us (70%)
  starting transfers between devices  24.7 us (18%)
  Pallas kernels  7.65 us (6%)
  waiting for transfers between devices  6.26 us (5%)
  other arithmetic  1.59 us (1%)
    all_to_all x7, blocking collectives, exchange(): return lax.all_to_all(values, axis, 0, 0, tiled=True)  96.7 us
    ppermute x4, starting transfers between devices, swap(): return lax.ppermute(values, PAIR, [(0, 1), (1, 0)])  20.9 us
    ppermute x2, waiting for transfers between devices, patch_swaps(): from_outer = lax.ppermute(outer, VERT, steps + [(b, a) for a, b in steps])  4.09 us
    ppermute x2, starting transfers between devices, patch_swaps(): from_outer = lax.ppermute(outer, VERT, steps + [(b, a) for a, b in steps])  3.84 us
  transfers between devices with their start and end apart: 6, of which 3 were waited for; matrix products, arithmetic and copies ran while one was open for 1% of the time, Pallas kernels for 2%

profile of v3, /device:TPU:1, one launch (start us, length us, event | category | flops | bytes accessed | tf_op | source)
XLA Modules:
  0.0 137.7 jit_solution(13633908085649167799)
XLA Ops:
  0.6 0.9 broadcast_select_fusion.2
  1.5 8.7 %collective-permute-start.1 = (bf16[2,64,256]{2,1,0:T(8,128)(2,1)S(1)}, bf16[2,64,256]{2,1,0:T(8,128)(2,1)S(1)}, u32[]{:S(2)}, u32[]{:S(2)}) collective-permute-start(bf16[2,64,256]{2,1,0:T(8,128)(2,1)S(1)} %get-tuple-element.43), channel_id=1, source_target_pairs={{0,1},{1,0},{2,3},{3,2},{4,5},{5,4},{6,7},{7,6},{8,9},{9,8},{10,11... | collective-permute-start | bytes 196616 | tf_op jit(solution)/shard_map/ppermute | solution.py:439
  10.3 1.9 %collective-permute-start = (bf16[2,64,256]{2,1,0:T(8,128)(2,1)S(1)}, bf16[2,64,256]{2,1,0:T(8,128)(2,1)S(1)}, u32[]{:S(2)}, u32[]{:S(2)}) collective-permute-start(bf16[2,64,256]{2,1,0:T(8,128)(2,1)S(1)} %get-tuple-element.44), channel_id=1, source_target_pairs={{1,2},{3,4},{5,6},{7,8},{9,10},{11,12},{13,14},{15,16},{17,18},{19... | collective-permute-start | bytes 196616 | tf_op jit(solution)/shard_map/ppermute | solution.py:433
  12.2 1.3 stage.1
  13.5 2.4 %collective-permute-done.outer_ref = bf16[2,64,256]{2,1,0:T(8,128)(2,1)S(1)} collective-permute-done((bf16[2,64,256]{2,1,0:T(8,128)(2,1)S(1)}, bf16[2,64,256]{2,1,0:T(8,128)(2,1)S(1)}, u32[]{:S(2)}, u32[]{:S(2)}) %collective-permute-start) | collective-permute-done | bytes 65568 | tf_op jit(solution)/shard_map/ppermute | solution.py:433
  15.9 0.7 conv_forward.1
  16.6 17.2 %all_to_all.35.came_ref = bf16[8,2,2,16,256]{4,3,2,1,0:T(8,128)(2,1)S(1)} all-to-all(bf16[8,2,2,16,256]{4,3,2,1,0:T(8,128)(2,1)S(1)} %get-tuple-element.26), channel_id=1, replica_groups=mesh['x_hi'=2,'x_lo'=2,'z_hi'=2,'y_hi'=4,'y_lo'=2,'z_mid'=2,'z_lo'=2,'co..., dimensions={0} | all-to-all | bytes 524288 | tf_op jit(solution)/shard_map/all_to_all | solution.py:419
  33.8 2.3 %attention.1 = (bf16[8,2,16,256]{3,2,1,0:T(8,128)(2,1)S(1)}, bf16[1024,256]{1,0:T(8,128)(2,1)S(1)}) custom-call(bf16[8,2,2,16,256]{4,3,2,1,0:T(8,128)(2,1)S(1)} %all_to_all.35.came_ref, bf16[4,256,256]{2,1,0:T(8,128)(2,1)S(1)} %copy-done), custom_call_target="tpu_custom_call" | custom-call | tf_op jit(solution)/shard_map/attention/pallas_call | solution.py:210
  36.1 12.3 %all_to_all.36.back_ref = bf16[8,2,16,256]{3,2,1,0:T(8,128)(2,1)S(1)} all-to-all(bf16[8,2,16,256]{3,2,1,0:T(8,128)(2,1)S(1)} %get-tuple-element.27), channel_id=1, replica_groups=mesh['x_hi'=2,'x_lo'=2,'z_hi'=2,'y_hi'=4,'y_lo'=2,'z_mid'=2,'z_lo'=2,'co..., dimensions={0} | all-to-all | bytes 262144 | tf_op jit(solution)/shard_map/all_to_all | solution.py:419
  48.4 1.2 conv_backward.1
  49.6 1.9 %collective-permute-start.4 = (bf16[8,176,256]{2,1,0:T(8,128)(2,1)S(1)}, bf16[8,176,256]{2,1,0:T(8,128)(2,1)S(1)}, u32[]{:S(2)}, u32[]{:S(2)}) collective-permute-start(bf16[8,176,256]{2,1,0:T(8,128)(2,1)S(1)} %get-tuple-element.36), channel_id=1, source_target_pairs={{0,1},{1,0},{2,3},{3,2},{4,5},{5,4},{6,7},{7,6},{8,9},{9,8},{10,11... | collective-permute-start | bytes 2162696 | tf_op jit(solution)/shard_map/ppermute | solution.py:439
  51.5 2.2 %collective-permute-done.4.came_ref = bf16[8,176,256]{2,1,0:T(8,128)(2,1)S(1)} collective-permute-done((bf16[8,176,256]{2,1,0:T(8,128)(2,1)S(1)}, bf16[8,176,256]{2,1,0:T(8,128)(2,1)S(1)}, u32[]{:S(2)}, u32[]{:S(2)}) %collective-permute-start.4) | collective-permute-done | bytes 720928 | tf_op jit(solution)/shard_map/ppermute | solution.py:439
  53.9 18.9 %all_to_all.37.came_ref = bf16[8,176,256]{2,1,0:T(8,128)(2,1)S(1)} all-to-all(bf16[8,176,256]{2,1,0:T(8,128)(2,1)S(1)} %pair_sum.1), channel_id=1, replica_groups=mesh['x_hi'=2,'x_lo'=2,'z_hi'=2,'y_hi'=4,'y_lo'=2,'z_mid'=2,'z_lo'=2,'co..., dimensions={0} | all-to-all | bytes 1441792 | tf_op jit(solution)/shard_map/all_to_all | solution.py:419
  72.9 10.6 %all_to_all.38 = bf16[24,16,128]{2,1,0:T(8,128)(2,1)S(1)} all-to-all(bf16[24,16,128]{2,1,0:T(8,128)(2,1)S(1)} %first_sum.1), channel_id=1, replica_groups=mesh['x_hi'=2,'x_lo'=2,'z_hi'=2,'y_hi'=4,'y_lo'=2,'z_mid'=2,'z_lo'=2,'co..., dimensions={0} | all-to-all | bytes 196608 | tf_op jit(solution)/shard_map/all_to_all | solution.py:419
  83.6 16.6 %all_to_all.39.came_ref = bf16[8,6,16,128]{3,2,1,0:T(8,128)(2,1)S(1)} all-to-all(bf16[8,6,16,128]{3,2,1,0:T(8,128)(2,1)S(1)} %shard_map.76), channel_id=1, replica_groups=mesh['x_hi'=2,'x_lo'=2,'z_hi'=2,'y_hi'=4,'y_lo'=2,'z_mid'=2,'z_lo'=2,'co..., dimensions={0} | all-to-all | bytes 393216 | tf_op jit(solution)/shard_map/all_to_all | solution.py:419
  100.2 9.4 %all_to_all.40.tiles_ref = bf16[24,16,128]{2,1,0:T(8,128)(2,1)S(1)} all-to-all(bf16[24,16,128]{2,1,0:T(8,128)(2,1)S(1)} %bitcast.6), channel_id=1, replica_groups=mesh['x_hi'=2,'x_lo'=2,'z_hi'=2,'y_hi'=4,'y_lo'=2,'z_mid'=2,'z_lo'=2,'co..., dimensions={0} | all-to-all | bytes 196608 | tf_op jit(solution)/shard_map/all_to_all | solution.py:419
  109.7 11.6 %all_to_all.41.own_ref = bf16[8,176,256]{2,1,0:T(8,128)(2,1)S(1)} all-to-all(bf16[8,176,256]{2,1,0:T(8,128)(2,1)S(1)} %untile.1), channel_id=1, replica_groups=mesh['x_hi'=2,'x_lo'=2,'z_hi'=2,'y_hi'=4,'y_lo'=2,'z_mid'=2,'z_lo'=2,'co..., dimensions={0} | all-to-all | bytes 1441792 | tf_op jit(solution)/shard_map/all_to_all | solution.py:419
  121.3 8.3 %collective-permute-start.5 = (bf16[8,176,256]{2,1,0:T(8,128)(2,1)S(1)}, bf16[8,176,256]{2,1,0:T(8,128)(2,1)S(1)}, u32[]{:S(2)}, u32[]{:S(2)}) collective-permute-start(bf16[8,176,256]{2,1,0:T(8,128)(2,1)S(1)} %all_to_all.41.own_ref), channel_id=1, source_target_pairs={{0,1},{1,0},{2,3},{3,2},{4,5},{5,4},{6,7},{7,6},{8,9},{9,8},{10,11... | collective-permute-start | bytes 2162696 | tf_op jit(solution)/shard_map/ppermute | solution.py:439
  129.6 1.9 %collective-permute-start.2 = (bf16[2,64,256]{2,1,0:T(8,128)(2,1)S(1)}, bf16[2,64,256]{2,1,0:T(8,128)(2,1)S(1)}, u32[]{:S(2)}, u32[]{:S(2)}) collective-permute-start(bf16[2,64,256]{2,1,0:T(8,128)(2,1)S(1)} %get-tuple-element.33), channel_id=1, source_target_pairs={{1,2},{3,4},{5,6},{7,8},{9,10},{11,12},{13,14},{15,16},{17,18},{19... | collective-permute-start | bytes 196616 | tf_op jit(solution)/shard_map/ppermute | solution.py:433
  131.6 1.9 %collective-permute-start.3 = (bf16[2,64,256]{2,1,0:T(8,128)(2,1)S(1)}, bf16[2,64,256]{2,1,0:T(8,128)(2,1)S(1)}, u32[]{:S(2)}, u32[]{:S(2)}) collective-permute-start(bf16[2,64,256]{2,1,0:T(8,128)(2,1)S(1)} %get-tuple-element.34), channel_id=1, source_target_pairs={{0,1},{1,0},{2,3},{3,2},{4,5},{5,4},{6,7},{7,6},{8,9},{9,8},{10,11... | collective-permute-start | bytes 196616 | tf_op jit(solution)/shard_map/ppermute | solution.py:439
  133.5 1.7 %collective-permute-done.2 = bf16[2,64,256]{2,1,0:T(8,128)(2,1)S(1)} collective-permute-done((bf16[2,64,256]{2,1,0:T(8,128)(2,1)S(1)}, bf16[2,64,256]{2,1,0:T(8,128)(2,1)S(1)}, u32[]{:S(2)}, u32[]{:S(2)}) %collective-permute-start.2) | collective-permute-done | bytes 65568 | tf_op jit(solution)/shard_map/ppermute | solution.py:433
  135.3 0.7 add_convert_fusion
  135.9 0.9 unpack_own.1
  136.8 0.9 unpack_other.1
  (11 shorter events, 0.4 us)
Async XLA Ops:
  1.5 12.0 %collective-permute-start.1 = (bf16[2,64,256]{2,1,0:T(8,128)(2,1)S(1)}, bf16[2,64,256]{2,1,0:T(8,128)(2,1)S(1)}, u32[]{:S(2)}, u32[]{:S(2)}) collective-permute-start(bf16[2,64,256]{2,1,0:T(8,128)(2,1)S(1)} %get-tuple-element.43), channel_id=1, source_target_pairs={{0,1},{1,0},{2,3},{3,2},{4,5},{5,4},{6,7},{7,6},{8,9},{9,8},{10,11... | collective-permute-start | bytes 196616 | tf_op jit(solution)/shard_map/ppermute | solution.py:439
  10.3 5.6 %collective-permute-start = (bf16[2,64,256]{2,1,0:T(8,128)(2,1)S(1)}, bf16[2,64,256]{2,1,0:T(8,128)(2,1)S(1)}, u32[]{:S(2)}, u32[]{:S(2)}) collective-permute-start(bf16[2,64,256]{2,1,0:T(8,128)(2,1)S(1)} %get-tuple-element.44), channel_id=1, source_target_pairs={{1,2},{3,4},{5,6},{7,8},{9,10},{11,12},{13,14},{15,16},{17,18},{19... | collective-permute-start | bytes 196616 | tf_op jit(solution)/shard_map/ppermute | solution.py:433
  16.6 17.2 %copy-start = (bf16[4,256,256]{2,1,0:T(8,128)(2,1)S(1)}, bf16[4,256,256]{2,1,0:T(8,128)(2,1)}, u32[]{:S(2)}) copy-start(bf16[4,256,256]{2,1,0:T(8,128)(2,1)} %w_ref.3) | copy-start | bytes 1572868
  49.6 4.1 %collective-permute-start.4 = (bf16[8,176,256]{2,1,0:T(8,128)(2,1)S(1)}, bf16[8,176,256]{2,1,0:T(8,128)(2,1)S(1)}, u32[]{:S(2)}, u32[]{:S(2)}) collective-permute-start(bf16[8,176,256]{2,1,0:T(8,128)(2,1)S(1)} %get-tuple-element.36), channel_id=1, source_target_pairs={{0,1},{1,0},{2,3},{3,2},{4,5},{5,4},{6,7},{7,6},{8,9},{9,8},{10,11... | collective-permute-start | bytes 2162696 | tf_op jit(solution)/shard_map/ppermute | solution.py:439
  121.3 15.5 %collective-permute-start.5 = (bf16[8,176,256]{2,1,0:T(8,128)(2,1)S(1)}, bf16[8,176,256]{2,1,0:T(8,128)(2,1)S(1)}, u32[]{:S(2)}, u32[]{:S(2)}) collective-permute-start(bf16[8,176,256]{2,1,0:T(8,128)(2,1)S(1)} %all_to_all.41.own_ref), channel_id=1, source_target_pairs={{0,1},{1,0},{2,3},{3,2},{4,5},{5,4},{6,7},{7,6},{8,9},{9,8},{10,11... | collective-permute-start | bytes 2162696 | tf_op jit(solution)/shard_map/ppermute | solution.py:439
  129.6 5.6 %collective-permute-start.2 = (bf16[2,64,256]{2,1,0:T(8,128)(2,1)S(1)}, bf16[2,64,256]{2,1,0:T(8,128)(2,1)S(1)}, u32[]{:S(2)}, u32[]{:S(2)}) collective-permute-start(bf16[2,64,256]{2,1,0:T(8,128)(2,1)S(1)} %get-tuple-element.33), channel_id=1, source_target_pairs={{1,2},{3,4},{5,6},{7,8},{9,10},{11,12},{13,14},{15,16},{17,18},{19... | collective-permute-start | bytes 196616 | tf_op jit(solution)/shard_map/ppermute | solution.py:433
  131.6 3.7 %collective-permute-start.3 = (bf16[2,64,256]{2,1,0:T(8,128)(2,1)S(1)}, bf16[2,64,256]{2,1,0:T(8,128)(2,1)S(1)}, u32[]{:S(2)}, u32[]{:S(2)}) collective-permute-start(bf16[2,64,256]{2,1,0:T(8,128)(2,1)S(1)} %get-tuple-element.34), channel_id=1, source_target_pairs={{0,1},{1,0},{2,3},{3,2},{4,5},{5,4},{6,7},{7,6},{8,9},{9,8},{10,11... | collective-permute-start | bytes 196616 | tf_op jit(solution)/shard_map/ppermute | solution.py:439
